TPU v7x, 32 devices: a whole 2x2x4 slice. The times are simulated.
32 devices in a mesh: dp: 4 (over y, x), seq: 4 (over z), tp: 2 (over core).
Axes of the slice: x: 2, y: 2, z: 4, core: 2. Of those that a mesh axis runs over, the one named last changes fastest.
Arguments:
- queries: bfloat16 [4, 2048, 5120], P('dp', 'seq', 'tp'), may hold values from -200 to 200
- keys: bfloat16 [4, 512, 5120], P('dp', None, 'tp'), may hold values from -6 to 6
- values: bfloat16 [4, 512, 5120], P('dp', None, 'tp'), may hold values from -6 to 6
- grad_attention: bfloat16 [4, 2048, 5120], P('dp', 'seq', 'tp'), may hold values from -48 to 48
- normed: bfloat16 [4, 512, 4096], P('dp', None, 'seq'), may hold values from -6 to 6
- norm_scale: float32 [4, 512], P('dp'), may hold values from 0.3 to 3
- norm_gain: float32 [4096], P('seq'), may hold values from 0.1 to 1.9
- key_weight: bfloat16 [4096, 5120], P('seq', 'tp'), may hold values from -0.078125 to 0.078125
- value_weight: bfloat16 [4096, 5120], P('seq', 'tp'), may hold values from -0.078125 to 0.078125
- key_down: bfloat16 [4096, 32], P('seq'), may hold values from -0.09375 to 0.09375
- key_up: bfloat16 [32, 5120], P(None, 'tp'), may hold values from -0.078125 to 0.078125
- value_down: bfloat16 [4096, 32], P('seq'), may hold values from -0.09375 to 0.09375
- value_up: bfloat16 [32, 5120], P(None, 'tp'), may hold values from -0.078125 to 0.078125
- out_weight: bfloat16 [10240, 4096], P('tp', 'seq'), may hold values from -0.09375 to 0.09375
Outputs:
- grad_queries: bfloat16 [4, 2048, 5120], P('dp', 'seq', 'tp')
- grad_text: bfloat16 [4, 512, 4096], P('dp', None, 'seq')
- grad_hidden: bfloat16 [4, 512, 10240], P('dp', 'seq', 'tp')
- grad_key_down: float32 [4096, 32], P('seq')
- grad_key_up: float32 [32, 5120], P(None, 'tp')
- grad_value_down: float32 [4096, 32], P('seq')
- grad_value_up: float32 [32, 5120], P(None, 'tp')
All inputs are finite; a program needn't handle non-finite values.
Results may differ from a plain program's by a relative error of at most 0.03.
Values may be sent and summed in bfloat16 or wider, within the bound.
A program may use at most 192 MiB of HBM per device.

v0:
```python
import jax
import jax.numpy as jnp
from jax import lax
from jax.sharding import PartitionSpec as P

HD = 128
DT = 4096


def contract_last(left_side, right_side):
    return lax.dot_general(
        left_side, right_side, (((1,), (1,)), ((), ())), preferred_element_type=jnp.float32
    )


def contract_first(left_side, right_side):
    return lax.dot_general(
        left_side, right_side, (((0,), (0,)), ((), ())), preferred_element_type=jnp.float32
    )


def attention_grads(queries, keys, values, grad_attention):
    row_count, columns = queries.shape
    length = keys.shape[0]
    head_count = columns // HD
    factor = HD ** (-0.5)
    query_heads = queries.reshape(row_count, head_count, HD)
    key_heads = keys.reshape(length, head_count, HD)
    value_heads = values.reshape(length, head_count, HD)
    grad_heads = grad_attention.reshape(row_count, head_count, HD)
    scores = (
        jnp.einsum("ihd,jhd->hij", query_heads, key_heads, preferred_element_type=jnp.float32)
        * factor
    )
    weights = jnp.exp(scores - jnp.max(scores, axis=2, keepdims=True))
    probability = weights / jnp.sum(weights, axis=2, keepdims=True)
    weights_low = probability.astype(jnp.bfloat16)
    grad_probs = jnp.einsum(
        "ihd,jhd->hij", grad_heads, value_heads, preferred_element_type=jnp.float32
    )
    grad_scores = probability * (
        grad_probs - jnp.sum(probability * grad_probs, axis=2, keepdims=True)
    )
    grad_low = grad_scores.astype(jnp.bfloat16)
    grad_query = (
        jnp.einsum("hij,jhd->ihd", grad_low, key_heads, preferred_element_type=jnp.float32) * factor
    )
    grad_key = (
        jnp.einsum("hij,ihd->jhd", grad_low, query_heads, preferred_element_type=jnp.float32)
        * factor
    )
    grad_value = jnp.einsum(
        "hij,ihd->jhd", weights_low, grad_heads, preferred_element_type=jnp.float32
    )
    return (
        grad_query.astype(jnp.bfloat16).reshape(row_count, columns),
        grad_key.reshape(length, columns),
        grad_value.reshape(length, columns),
    )


def norm_backward(
    context_base, key_back, value_back, text_rows, scale_rows, norm_gain, key_down, value_down
):
    grad_context = (
        context_base + contract_last(key_back, key_down) + contract_last(value_back, value_down)
    )
    text_values = text_rows.astype(jnp.float32)
    scaled = norm_gain * grad_context
    local_sum = jnp.sum(text_values * scaled, axis=1)
    token_sum = lax.psum(local_sum, "seq")
    return (scale_rows[:, None] * (scaled - text_values * (token_sum / DT)[:, None])).astype(
        jnp.bfloat16
    )


def shards(
    queries,
    keys,
    values,
    grad_attention,
    normed,
    norm_scale,
    norm_gain,
    key_weight,
    value_weight,
    key_down,
    key_up,
    value_down,
    value_up,
    out_weight,
):
    grad_query, grad_key, grad_value = attention_grads(
        queries[0], keys[0], values[0], grad_attention[0]
    )
    context = (normed[0].astype(jnp.float32) * norm_gain).astype(jnp.bfloat16)
    key_part = jnp.dot(context, key_down, preferred_element_type=jnp.float32)
    value_part = jnp.dot(context, value_down, preferred_element_type=jnp.float32)
    key_sum, value_sum, key_lowsum, value_lowsum = (
        lax.psum(grad_key.astype(jnp.bfloat16), "seq").astype(jnp.float32),
        lax.psum(grad_value.astype(jnp.bfloat16), "seq").astype(jnp.float32),
        lax.psum(key_part.astype(jnp.bfloat16), "seq").astype(jnp.float32),
        lax.psum(value_part.astype(jnp.bfloat16), "seq").astype(jnp.float32),
    )
    key_grad = key_sum.astype(jnp.bfloat16)
    value_grad = value_sum.astype(jnp.bfloat16)
    key_latent = key_lowsum.astype(jnp.bfloat16)
    value_latent = value_lowsum.astype(jnp.bfloat16)
    key_project = contract_last(key_grad, key_up)
    value_project = contract_last(value_grad, value_up)
    context_part = contract_last(key_grad, key_weight) + contract_last(value_grad, value_weight)
    context_base, key_total, value_total = (
        lax.psum(context_part.astype(jnp.bfloat16), "tp").astype(jnp.float32),
        lax.psum(key_project.astype(jnp.bfloat16), "tp").astype(jnp.float32),
        lax.psum(value_project.astype(jnp.bfloat16), "tp").astype(jnp.float32),
    )
    key_back = key_total.astype(jnp.bfloat16)
    value_back = value_total.astype(jnp.bfloat16)
    grad_text = norm_backward(
        context_base,
        key_back,
        value_back,
        normed[0],
        norm_scale[0],
        norm_gain,
        key_down,
        value_down,
    )
    prompt_count = lax.axis_size("dp")
    down_key = contract_first(context, key_back)
    down_value = contract_first(context, value_back)
    up_key = contract_first(key_latent, key_grad)
    up_value = contract_first(value_latent, value_grad)
    down_key, up_key, down_value, up_value = (
        lax.psum(down_key.astype(jnp.bfloat16), "dp").astype(jnp.float32),
        lax.psum(up_key.astype(jnp.bfloat16), "dp").astype(jnp.float32),
        lax.psum(down_value.astype(jnp.bfloat16), "dp").astype(jnp.float32),
        lax.psum(up_value.astype(jnp.bfloat16), "dp").astype(jnp.float32),
    )
    grad_hidden = lax.psum_scatter(
        contract_last(grad_text, out_weight).astype(jnp.bfloat16),
        "seq",
        scatter_dimension=0,
        tiled=True,
    )
    return (
        grad_query[None],
        grad_text[None],
        grad_hidden[None],
        down_key / prompt_count,
        up_key / prompt_count,
        down_value / prompt_count,
        up_value / prompt_count,
    )


def solution(mesh):
    return jax.shard_map(
        shards,
        mesh=mesh,
        in_specs=(
            P("dp", "seq", "tp"),
            P("dp", None, "tp"),
            P("dp", None, "tp"),
            P("dp", "seq", "tp"),
            P("dp", None, "seq"),
            P("dp", None),
            P("seq"),
            P("seq", "tp"),
            P("seq", "tp"),
            P("seq", None),
            P(None, "tp"),
            P("seq", None),
            P(None, "tp"),
            P("tp", "seq"),
        ),
        out_specs=(
            P("dp", "seq", "tp"),
            P("dp", None, "seq"),
            P("dp", "seq", "tp"),
            P("seq", None),
            P(None, "tp"),
            P("seq", None),
            P(None, "tp"),
        ),
        check_vma=False,
    )
```

profile of v0, /device:TPU:0, one launch (start us, length us, event | category | flops | bytes accessed | tf_op | source)
XLA Modules:
  0.0 517.3 jit_solution(190219239213551095)
XLA Ops:
  7.2 0.0 all-reduce.14.cloned.1.call-start
  7.2 4.4 copy.32
  11.6 3.0 copy.33
  14.6 4.4 copy.36
  19.0 4.4 copy.37
  23.4 12.1 %fusion.22 = (f32[20,512]{1,0:T(8,128)S(1)}, f32[20,512,512]{1,2,0:T(8,128)}) fusion(bf16[512,20,128]{0,2,1:T(8,128)(2,1)} %bitcast.63, bf16[512,20,128]{0,2,1:T(8,128)(2,1)S(1)} %bitcast.58), kind=kOutput, calls=%fused_computation.39 | convolution fusion | flops 1357906432 | bytes 26255360 | tf_op jit(solution)/shard_map/sub | solution.py:35
  35.5 10.9 %fusion.14 = bf16[20,512,128]{1,2,0:T(8,128)(2,1)} fusion(bf16[512,20,128]{0,2,1:T(8,128)(2,1)} %bitcast.65, f32[20,512,512]{1,2,0:T(8,128)} %get-tuple-element.32, f32[20,512]{1,0:T(8,128)S(1)} %get-tuple-element.31), kind=kOutput, calls=%fused_computation.26 | convolution fusion | flops 1353973760 | bytes 26255360 | tf_op jit(solution)/shard_map/hij,ihd->jhd/dot_general | solution.py:52
  46.5 15.6 %multiply_reduce_fusion = (f32[20,512]{1,0:T(8,128)S(1)}, f32[20,512,512]{1,2,0:T(8,128)}) fusion(f32[20,512,512]{1,2,0:T(8,128)} %get-tuple-element.32, f32[20,512]{1,0:T(8,128)S(1)} %get-tuple-element.31, bf16[512,20,128]{0,2,1:T(8,128)(2,1)} %bitcast.66, bf16[512,20,128]{0,2,1:T(8,128)(2,1)} %bitcast.67), kind=kOutput, calls=%fused_computation.2 | convolution fusion | flops 1357895680 | bytes 47267840 | tf_op jit(solution)/shard_map/ihd,jhd->hij/dot_general | solution.py:38
  62.1 18.7 %multiply_convert_fusion = bf16[20,512,512]{1,2,0:T(8,128)(2,1)} fusion(f32[20,512,512]{1,2,0:T(8,128)} %get-tuple-element.34, f32[20,512]{1,0:T(8,128)S(1)} %get-tuple-element.33, f32[20,512,512]{1,2,0:T(8,128)} %get-tuple-element.32, f32[20,512]{1,0:T(8,128)S(1)} %get-tuple-element.31), kind=kLoop, calls=%fused_computation.1 | loop fusion | flops 20971520 | bytes 52510720 | tf_op jit(solution)/shard_map/convert_element_type | solution.py:44
  80.8 9.7 %multiply_convert_fusion.1 = bf16[20,512,128]{1,2,0:T(8,128)(2,1)} fusion(bf16[20,512,512]{1,2,0:T(8,128)(2,1)} %multiply_convert_fusion, bf16[512,20,128]{0,2,1:T(8,128)(2,1)} %bitcast.64), kind=kOutput, calls=%fused_computation.11 | convolution fusion | flops 1344798720 | bytes 15728640 | tf_op jit(solution)/shard_map/hij,ihd->jhd/dot_general | solution.py:49
  90.5 0.0 all-reduce.14.cloned.1.call-update
  90.6 0.0 all-reduce.12.cloned.1.call-start
  90.6 0.8 copy-done.7
  91.4 2.3 convolution_convert_fusion.3
  93.7 2.3 convolution_convert_fusion.4
  96.0 0.0 all-reduce.12.cloned.1.call-update
  96.0 0.2 all-reduce.18.cloned.1.call-start
  96.2 186.2 %all-reduce.14.cloned.1.call-done = (bf16[512,2560]{0,1:T(8,128)(2,1)}, bf16[512,2560]{0,1:T(8,128)(2,1)}) async-done(((bf16[512,2560]{0,1:T(8,128)(2,1)}, bf16[512,2560]{0,1:T(8,128)(2,1)}), (bf16[512,2560]{0,1:T(8,128)(2,1)}, bf16[512,2560]{0,1:T(8,128)(2,1)})) %all-reduce.14.cloned.1.call-update) | async-done | bytes 5242896 | tf_op jit(solution)/shard_map/psum | solution.py:100
  282.4 3.1 convolution_convert_fusion.7
  285.5 5.1 fusion.23
  290.6 6.4 %add_convert_fusion = bf16[512,1024]{1,0:T(8,128)(2,1)} fusion(f32[512,1024]{1,0:T(8,128)S(1)} %fusion.23, bf16[512,2560]{0,1:T(8,128)(2,1)S(1)} %copy-done.2, bf16[1024,2560]{1,0:T(8,128)(2,1)} %param.22), kind=kOutput, calls=%fused_computation.25 | convolution fusion | flops 2685403136 | bytes 11010048 | tf_op jit(solution)/shard_map/dot_general | solution.py:11
  297.0 2.9 convolution_convert_fusion.8
  299.9 0.0 all-reduce.18.cloned.1.call-update
  299.9 0.0 all-reduce.10.cloned.1.call-start
  300.0 20.0 %all-reduce.12.cloned.1.call-done = (bf16[512,32]{1,0:T(8,128)(2,1)}, bf16[512,32]{1,0:T(8,128)(2,1)}) async-done(((bf16[512,32]{1,0:T(8,128)(2,1)}, bf16[512,32]{1,0:T(8,128)(2,1)}), (bf16[512,32]{1,0:T(8,128)(2,1)}, bf16[512,32]{1,0:T(8,128)(2,1)})) %all-reduce.12.cloned.1.call-update) | async-done | bytes 65552 | tf_op jit(solution)/shard_map/psum | solution.py:102
  320.0 3.4 convolution_convert_fusion.1
  323.4 0.0 all-reduce.10.cloned.1.call-update
  323.4 0.0 all-reduce.16.cloned.1.call-start
  323.5 3.3 convolution_convert_fusion.2
  326.8 13.7 %all-reduce.18.cloned.1.call-done = (bf16[512,32]{0,1:T(8,128)(2,1)}, bf16[512,32]{0,1:T(8,128)(2,1)}) async-done(((bf16[512,32]{0,1:T(8,128)(2,1)}, bf16[512,32]{0,1:T(8,128)(2,1)}), (bf16[512,32]{0,1:T(8,128)(2,1)}, bf16[512,32]{0,1:T(8,128)(2,1)})) %all-reduce.18.cloned.1.call-update) | async-done | bytes 65552 | tf_op jit(solution)/shard_map/psum | solution.py:114
  340.5 2.2 convolution_convert_fusion.5
  342.7 2.2 convolution_convert_fusion.6
  344.9 2.5 fusion.24
  347.4 0.0 all-reduce.16.cloned.1.call-update
  347.5 0.0 reduce-scatter.2.cloned.1.call-start
  347.5 16.4 %all-reduce.10.cloned.1.call-done = bf16[512,1024]{1,0:T(8,128)(2,1)} async-done(((bf16[512,1024]{1,0:T(8,128)(2,1)}), bf16[512,1024]{1,0:T(8,128)(2,1)}) %all-reduce.10.cloned.1.call-update) | async-done | bytes 1048592 | tf_op jit(solution)/shard_map/psum | solution.py:113
  363.9 4.1 fusion.9
  368.0 12.2 %psum.89 = f32[512]{0:T(512)S(1)} all-reduce(f32[512]{0:T(512)S(1)} %get-tuple-element.35), channel_id=1, replica_groups=mesh['dp'=4,'seq'=4,'tp'=2] {'seq'}, use_global_device_ids=true, to_apply=%region_9.0 | all-reduce | flops 512 | bytes 4096 | tf_op jit(solution)/shard_map/psum | solution.py:71
  380.2 2.2 fusion.12
  382.5 1.0 copy-done.3
  383.4 11.4 %convolution_convert_fusion = bf16[512,5120]{1,0:T(8,128)(2,1)} fusion(bf16[512,1024]{1,0:T(8,128)(2,1)S(1)} %fusion.12, bf16[5120,1024]{1,0:T(8,128)(2,1)} %param.27), kind=kOutput, calls=%fused_computation.10 | convolution fusion | flops 5371330560 | bytes 16777216 | tf_op jit(solution)/shard_map/dot_general | solution.py:11
  394.8 0.0 reduce-scatter.2.cloned.1.call-update
  394.8 7.1 %multiply_convert_fusion.2 = bf16[20,512,128]{1,2,0:T(8,128)(2,1)} fusion(bf16[512,20,128]{0,2,1:T(8,128)(2,1)S(1)} %bitcast.59, bf16[20,512,512]{1,2,0:T(8,128)(2,1)} %multiply_convert_fusion), kind=kOutput, calls=%fused_computation.12 | convolution fusion | flops 1344798720 | bytes 15728640 | tf_op jit(solution)/shard_map/hij,jhd->ihd/dot_general | solution.py:46
  402.0 4.4 copy.43
  406.3 7.6 %all-reduce.16.cloned.1.call-done = (bf16[1024,32]{0,1:T(8,128)(2,1)}, bf16[32,2560]{1,0:T(8,128)(2,1)}, bf16[1024,32]{0,1:T(8,128)(2,1)}, bf16[32,2560]{1,0:T(8,128)(2,1)}) async-done(((bf16[1024,32]{0,1:T(8,128)(2,1)}, bf16[32,2560]{1,0:T(8,128)(2,1)}, bf16[1024,32]{0,1:T(8,128)(2,1)}, bf16[32,2560]{1,0:T(8,128)(2,1)}), (bf16[1024,32]{0,1:T(8,128)(2,1)}, bf16[32,2560]{1,0:T(8,128)(2,1)}, ...) | async-done | bytes 458768 | tf_op jit(solution)/shard_map/psum | solution.py:135
  413.9 1.6 convert_multiply_fusion.5
  415.5 1.9 convert_multiply_fusion.3
  417.4 93.1 %reduce-scatter.2.cloned.1.call-done = bf16[128,5120]{1,0:T(8,128)(2,1)} async-done(((bf16[512,5120]{1,0:T(8,128)(2,1)}), bf16[128,5120]{1,0:T(8,128)(2,1)}) %reduce-scatter.2.cloned.1.call-update) | async-done | bytes 1310736 | tf_op jit(solution)/shard_map/reduce_scatter | solution.py:140
  (21 shorter events, 0.1 us)
Async XLA Ops:
  7.2 275.2 %copy-start = (bf16[32,2560]{1,0:T(8,128)(2,1)S(1)}, bf16[32,2560]{1,0:T(8,128)(2,1)}, u32[]{:S(2)}) copy-start(bf16[32,2560]{1,0:T(8,128)(2,1)} %param.26) | copy-start | bytes 491524
  7.2 275.2 %all-reduce.14.cloned.1.call-start = ((), (), s32[]{:S(2)}) async-start(), calls=%async_computation.4 | async-start | bytes 10485760 | tf_op jit(solution)/shard_map/psum | solution.py:100
  90.5 0.8 copy-start.7
  90.5 0.8 copy-start.9
  90.5 3.1 copy-start.8
  90.6 229.4 %all-reduce.12.cloned.1.call-start = ((), (), s32[]{:S(2)}) async-start(), calls=%async_computation.3 | async-start | bytes 524288 | tf_op jit(solution)/shard_map/psum | solution.py:102
  96.0 244.5 %all-reduce.18.cloned.1.call-start = ((), (), s32[]{:S(2)}) async-start(), calls=%async_computation.6 | async-start | bytes 131072 | tf_op jit(solution)/shard_map/psum | solution.py:114
  282.4 3.1 copy-start.1
  285.5 5.1 copy-start.2
  290.5 6.4 %copy-start.4 = (bf16[32,2560]{1,0:T(8,128)(2,1)S(1)}, bf16[32,2560]{1,0:T(8,128)(2,1)}, u32[]{:S(2)}) copy-start(bf16[32,2560]{1,0:T(8,128)(2,1)} %param.24) | copy-start | bytes 491524
  299.9 64.0 %all-reduce.10.cloned.1.call-start = ((), (), s32[]{:S(2)}) async-start(), calls=%async_computation.1 | async-start | bytes 2097152 | tf_op jit(solution)/shard_map/psum | solution.py:113
  320.0 3.5 copy-start.6
  323.4 90.5 %all-reduce.16.cloned.1.call-start = ((), (), s32[]{:S(2)}) async-start(), calls=%async_computation.5 | async-start | bytes 917504 | tf_op jit(solution)/shard_map/psum | solution.py:135
  340.5 23.4 %copy-start.5 = (bf16[512,32]{0,1:T(8,128)(2,1)S(1)}, bf16[512,32]{0,1:T(8,128)(2,1)}, u32[]{:S(2)}) copy-start(bf16[512,32]{0,1:T(8,128)(2,1)} %get-tuple-element.30) | copy-start | bytes 98308
  347.4 32.8 %copy-start.10 = (f32[1,512]{1,0:T(1,128)S(1)}, f32[1,512]{1,0:T(1,128)}, u32[]{:S(2)}) copy-start(f32[1,512]{1,0:T(1,128)} %param.19) | copy-start | bytes 6148
  347.5 163.0 %reduce-scatter.2.cloned.1.call-start = ((), (), s32[]{:S(2)}) async-start(), calls=%async_computation.2 | async-start | bytes 6553600 | tf_op jit(solution)/shard_map/reduce_scatter | solution.py:140
  382.4 1.0 copy-start.3
Sparse Core Ops, SparseCore 0:
  90.7 191.6 all-reduce.13
  285.3 34.6 all-reduce.11
  322.9 17.5 all-reduce.17
  343.2 20.6 all-reduce.9
  367.6 46.3 all-reduce.15
  416.7 93.7 reduce-scatter.1
where the time goes:
time: 518 us; the launch traced here: 517 us
  waiting for transfers between devices  337 us (65%)
  matrix products  107 us (21%)
  other arithmetic  24.4 us (5%)
  local copies, waits for them, and re-layouts  22.3 us (4%)
  between operations  14.2 us (3%)
  blocking collectives  12.2 us (2%)
    psum x1, waiting for transfers between devices, shards(): lax.psum(grad_key.astype(jnp.bfloat16), 'seq').astype(jnp.float32)  186 us
    reduce_scatter x1, waiting for transfers between devices, shards(): lax.psum_scatter(contract_last(grad_text, out_weight).astype(jnp.bfloat16...  93.1 us
    dot_general x7, matrix products, contract_last(): lax.dot_general(left_side, right_side, (((1,), (1,)), ((), ())), preferre...  35.5 us
    unnamed x27, local copies, waits for them, and re-layouts  22.3 us
    psum x1, waiting for transfers between devices, shards(): lax.psum(key_part.astype(jnp.bfloat16), 'seq').astype(jnp.float32)  20 us
    convert_element_type x1, other arithmetic, attention_grads(): grad_low = grad_scores.astype(jnp.bfloat16)  18.7 us
    psum x1, waiting for transfers between devices, shards(): lax.psum(context_part.astype(jnp.bfloat16), 'tp').astype(jnp.float32)  16.4 us
    dot_general x1, matrix products, attention_grads(): jnp.einsum('ihd,jhd->hij', grad_heads, value_heads, preferred_element_typ...  15.6 us
  transfers between devices with their start and end apart: 6, of which 6 were waited for; matrix products, arithmetic and copies ran while one was open for 13% of the time, Pallas kernels for 0%

commit v1 on v0

v1 whole, which is shorter than its diff:
```python
import functools

import jax
import jax.numpy as jnp
from jax import lax
from jax.experimental import pallas as pl
from jax.experimental.pallas import tpu as pltpu
from jax.sharding import PartitionSpec as P

HD = 128
DT = 4096
MESH = pl.DeviceIdType.MESH


def contract_last(left_side, right_side):
    return lax.dot_general(
        left_side, right_side, (((1,), (1,)), ((), ())), preferred_element_type=jnp.float32
    )


def contract_first(left_side, right_side):
    return lax.dot_general(
        left_side, right_side, (((0,), (0,)), ((), ())), preferred_element_type=jnp.float32
    )


def dot(left_side, right_side, left_dim, right_dim):
    return lax.dot_general(
        left_side,
        right_side,
        (((left_dim,), (right_dim,)), ((), ())),
        preferred_element_type=jnp.float32,
    )


def attention_kernel(
    n,
    heads,
    lag,
    queries,
    keys,
    values,
    grads,
    key_weight,
    value_weight,
    key_up,
    value_up,
    grad_query,
    key_grad,
    value_grad,
    context,
    key_project,
    value_project,
    part,
    up_in,
    up_out,
    down_in,
    down_out,
    total,
    key_total,
    value_total,
    up_send,
    up_recv,
    down_send,
    down_recv,
):
    step = pl.program_id(0)
    me = lax.axis_index("seq")
    factor = HD ** (-0.5)
    has_low = me > 0
    has_high = me < n - 1

    def up_copy(chunk, source):
        return pltpu.make_async_remote_copy(
            src_ref=source.at[chunk],
            dst_ref=up_in.at[chunk],
            send_sem=up_send.at[chunk],
            recv_sem=up_recv.at[chunk],
            device_id={"seq": lax.rem(me + 1, n)},
            device_id_type=MESH,
        )

    def down_copy(chunk, source):
        return pltpu.make_async_remote_copy(
            src_ref=source.at[chunk],
            dst_ref=down_in.at[chunk],
            send_sem=down_send.at[chunk],
            recv_sem=down_recv.at[chunk],
            device_id={"seq": lax.rem(me + n - 1, n)},
            device_id_type=MESH,
        )

    @pl.when(step == 0)
    def _():
        barrier = pltpu.get_barrier_semaphore()

        @pl.when(has_low)
        def _():
            pl.semaphore_signal(
                barrier,
                inc=1,
                device_id={"seq": lax.rem(me + n - 1, n)},
                device_id_type=MESH,
            )

        @pl.when(has_high)
        def _():
            pl.semaphore_signal(
                barrier, inc=1, device_id={"seq": lax.rem(me + 1, n)}, device_id_type=MESH
            )

        total[...] = jnp.zeros_like(total)
        key_total[...] = jnp.zeros_like(key_total)
        value_total[...] = jnp.zeros_like(value_total)

        pl.semaphore_wait(barrier, has_low.astype(jnp.int32) + has_high.astype(jnp.int32))

    @pl.when(step < heads)
    def _():
        query, key, value, grad = queries[...], keys[...], values[...], grads[...]
        scores = dot(key, query, 1, 1) * factor
        weights = jnp.exp(scores - jnp.max(scores, axis=0, keepdims=True))
        probability = weights * (1.0 / jnp.sum(weights, axis=0, keepdims=True))
        part[step, :, HD:] = dot(probability.astype(jnp.bfloat16), grad, 1, 0).astype(jnp.bfloat16)
        grad_probs = dot(value, grad, 1, 1)
        grad_scores = probability * (
            grad_probs - jnp.sum(probability * grad_probs, axis=0, keepdims=True)
        )
        grad_low = grad_scores.astype(jnp.bfloat16)
        part[step, :, :HD] = (dot(grad_low, query, 1, 0) * factor).astype(jnp.bfloat16)
        grad_query[...] = (dot(grad_low, key, 0, 0) * factor).astype(jnp.bfloat16)

    up_chunk = step - me
    up_live = jnp.logical_and(up_chunk >= 0, up_chunk < heads)

    @pl.when(jnp.logical_and(up_live, has_low))
    def _():
        up_copy(up_chunk, up_out).wait_recv()

        @pl.when(has_high)
        def _():
            up_out[up_chunk] = up_in[up_chunk] + part[up_chunk]
            up_copy(up_chunk, up_out).start()

    @pl.when(jnp.logical_and(up_live, me == 0))
    def _():
        up_copy(up_chunk, part).start()
        up_in[up_chunk] = jnp.zeros(up_in.shape[1:], up_in.dtype)

    down_chunk = step - (n - 1 - me)
    down_live = jnp.logical_and(down_chunk >= 0, down_chunk < heads)

    @pl.when(jnp.logical_and(down_live, has_high))
    def _():
        down_copy(down_chunk, down_out).wait_recv()

        @pl.when(has_low)
        def _():
            down_out[down_chunk] = down_in[down_chunk] + part[down_chunk]
            down_copy(down_chunk, down_out).start()

    @pl.when(jnp.logical_and(down_live, me == n - 1))
    def _():
        down_copy(down_chunk, part).start()
        down_in[down_chunk] = jnp.zeros(down_in.shape[1:], down_in.dtype)

    @pl.when(step >= lag)
    def _():
        chunk = step - lag

        @pl.when(has_high)
        def _():
            up_copy(chunk, up_out).wait_send()

        @pl.when(has_low)
        def _():
            down_copy(chunk, down_out).wait_send()

        both = (
            up_in[chunk].astype(jnp.float32)
            + part[chunk].astype(jnp.float32)
            + down_in[chunk].astype(jnp.float32)
        ).astype(jnp.bfloat16)
        key_grad[...] = both[:, :HD]
        value_grad[...] = both[:, HD:]
        slab = jnp.concatenate([key_weight[...], value_weight[...]], axis=1)
        total[...] += dot(both, slab, 1, 1)
        key_total[...] += dot(both[:, :HD], key_up[...], 1, 1)
        value_total[...] += dot(both[:, HD:], value_up[...], 1, 1)

    @pl.when(step == heads + lag - 1)
    def _():
        context[...] = total[...].astype(jnp.bfloat16)
        key_project[...] = key_total[...].astype(jnp.bfloat16)
        value_project[...] = value_total[...].astype(jnp.bfloat16)


def attention_grads(
    queries, keys, values, grad_attention, key_weight, value_weight, key_up, value_up
):
    rows, columns = queries.shape
    length = keys.shape[0]
    features = key_weight.shape[0]
    rank = key_up.shape[0]
    heads = columns // HD
    n = lax.axis_size("seq")
    lag = n + 1

    def early(height):
        return pl.BlockSpec((height, HD), lambda step: (0, jnp.minimum(step, heads - 1)))

    def late(height):
        return pl.BlockSpec((height, HD), lambda step: (0, jnp.maximum(step - lag, 0)))

    def fixed(height, width):
        return pl.BlockSpec((height, width), lambda step: (0, 0))

    buffer = pltpu.VMEM((heads, length, 2 * HD), jnp.bfloat16)
    semaphores = pltpu.SemaphoreType.DMA((heads,))
    return pl.pallas_call(
        functools.partial(attention_kernel, n, heads, lag),
        grid=(heads + lag,),
        out_shape=(
            jax.ShapeDtypeStruct((rows, columns), jnp.bfloat16),
            jax.ShapeDtypeStruct((length, columns), jnp.bfloat16),
            jax.ShapeDtypeStruct((length, columns), jnp.bfloat16),
            jax.ShapeDtypeStruct((length, features), jnp.bfloat16),
            jax.ShapeDtypeStruct((length, rank), jnp.bfloat16),
            jax.ShapeDtypeStruct((length, rank), jnp.bfloat16),
        ),
        in_specs=[
            early(rows),
            early(length),
            early(length),
            early(rows),
            late(features),
            late(features),
            late(rank),
            late(rank),
        ],
        out_specs=(
            early(rows),
            late(length),
            late(length),
            fixed(length, features),
            fixed(length, rank),
            fixed(length, rank),
        ),
        scratch_shapes=[buffer] * 5
        + [
            pltpu.VMEM((length, features), jnp.float32),
            pltpu.VMEM((length, rank), jnp.float32),
            pltpu.VMEM((length, rank), jnp.float32),
        ]
        + [semaphores] * 4,
        compiler_params=pltpu.CompilerParams(
            collective_id=0, has_side_effects=True, vmem_limit_bytes=50 * 1024 * 1024
        ),
        cost_estimate=pl.CostEstimate(
            flops=14 * rows * length * columns,
            bytes_accessed=12 * rows * columns,
            transcendentals=rows * length * heads,
        ),
        name="attention",
    )(queries, keys, values, grad_attention, key_weight, value_weight, key_up, value_up)


def norm_backward(
    context_base, key_back, value_back, text_rows, scale_rows, norm_gain, key_down, value_down
):
    grad_context = (
        context_base + contract_last(key_back, key_down) + contract_last(value_back, value_down)
    )
    text_values = text_rows.astype(jnp.float32)
    scaled = norm_gain * grad_context
    local_sum = jnp.sum(text_values * scaled, axis=1)
    token_sum = lax.psum(local_sum, "seq")
    return (scale_rows[:, None] * (scaled - text_values * (token_sum / DT)[:, None])).astype(
        jnp.bfloat16
    )


def shards(
    queries,
    keys,
    values,
    grad_attention,
    normed,
    norm_scale,
    norm_gain,
    key_weight,
    value_weight,
    key_down,
    key_up,
    value_down,
    value_up,
    out_weight,
):
    context = (normed[0].astype(jnp.float32) * norm_gain).astype(jnp.bfloat16)
    latent_part = jnp.concatenate(
        [
            jnp.dot(context, key_down, preferred_element_type=jnp.float32),
            jnp.dot(context, value_down, preferred_element_type=jnp.float32),
        ],
        axis=1,
    )
    latent = lax.psum(latent_part.astype(jnp.bfloat16), "seq")
    grad_query, key_grad, value_grad, context_part, key_project, value_project = attention_grads(
        queries[0],
        keys[0],
        values[0],
        grad_attention[0],
        key_weight,
        value_weight,
        key_up,
        value_up,
    )
    context_base, key_total, value_total = (
        lax.psum(context_part, "tp").astype(jnp.float32),
        lax.psum(key_project, "tp").astype(jnp.float32),
        lax.psum(value_project, "tp").astype(jnp.float32),
    )
    key_back = key_total.astype(jnp.bfloat16)
    value_back = value_total.astype(jnp.bfloat16)
    grad_text = norm_backward(
        context_base,
        key_back,
        value_back,
        normed[0],
        norm_scale[0],
        norm_gain,
        key_down,
        value_down,
    )
    prompt_count = lax.axis_size("dp")
    down_key = contract_first(context, key_back)
    down_value = contract_first(context, value_back)
    rank = key_down.shape[1]
    block = key_grad.shape[0] // lax.axis_size("seq")
    start = lax.axis_index("seq") * block
    latent_block = lax.dynamic_slice_in_dim(latent, start, block, 0)
    up_key = contract_first(
        latent_block[:, :rank], lax.dynamic_slice_in_dim(key_grad, start, block, 0)
    )
    up_value = contract_first(
        latent_block[:, rank:], lax.dynamic_slice_in_dim(value_grad, start, block, 0)
    )
    down_key, down_value = (
        lax.psum(down_key.astype(jnp.bfloat16), "dp").astype(jnp.float32),
        lax.psum(down_value.astype(jnp.bfloat16), "dp").astype(jnp.float32),
    )
    up_key, up_value = (
        lax.psum(up_key.astype(jnp.bfloat16), ("dp", "seq")).astype(jnp.float32),
        lax.psum(up_value.astype(jnp.bfloat16), ("dp", "seq")).astype(jnp.float32),
    )
    grad_hidden = lax.psum_scatter(
        contract_last(grad_text, out_weight).astype(jnp.bfloat16),
        "seq",
        scatter_dimension=0,
        tiled=True,
    )
    return (
        grad_query[None],
        grad_text[None],
        grad_hidden[None],
        down_key / prompt_count,
        up_key / prompt_count,
        down_value / prompt_count,
        up_value / prompt_count,
    )


def solution(mesh):
    return jax.shard_map(
        shards,
        mesh=mesh,
        in_specs=(
            P("dp", "seq", "tp"),
            P("dp", None, "tp"),
            P("dp", None, "tp"),
            P("dp", "seq", "tp"),
            P("dp", None, "seq"),
            P("dp", None),
            P("seq"),
            P("seq", "tp"),
            P("seq", "tp"),
            P("seq", None),
            P(None, "tp"),
            P("seq", None),
            P(None, "tp"),
            P("tp", "seq"),
        ),
        out_specs=(
            P("dp", "seq", "tp"),
            P("dp", None, "seq"),
            P("dp", "seq", "tp"),
            P("seq", None),
            P(None, "tp"),
            P("seq", None),
            P(None, "tp"),
        ),
        check_vma=False,
    )
```

time: 518 us -> 500 us (0.965)
  Pallas kernels: 0 us -> 148 us
  matrix products: 107 us -> 24.2 us
  waiting for transfers between devices: 337 us -> 291 us
  other arithmetic: 24.4 us -> 4.5 us
  local copies, waits for them, and re-layouts: 22.3 us -> 4.33 us
    pallas_call x0 -> x1, Pallas kernels: none -> 148 us  [attention_grads(): pl.pallas_call(functools.partial(attention_kernel, n, heads, lag), grid=(...]
    psum x4, waiting for transfers between devices: 236 us -> 177 us  [the longest x1 113 us: shards(): lax.psum(up_key.astype(jnp.bfloat16), ('dp', 'seq')).astype(jnp.float32)]
    dot_general x5 -> x1, matrix products: 45.7 us -> 0.41 us  [shards(): jnp.dot(context, key_down, preferred_element_type=jnp.float32)]
    dot_general x7 -> x3, matrix products: 35.5 us -> 15.6 us  [contract_last(): lax.dot_general(left_side, right_side, (((1,), (1,)), ((), ())), preferre...]
    convert_element_type x1 -> x0, other arithmetic: 18.7 us -> none  [attention_grads(): grad_low = grad_scores.astype(jnp.bfloat16)]
    unnamed x27 -> x23, local copies, waits for them, and re-layouts: 22.3 us -> 4.33 us
    sub x1 -> x0, matrix products: 12.1 us -> none  [attention_grads(): weights = jnp.exp(scores - jnp.max(scores, axis=2, keepdims=True))]
    psum x1, waiting for transfers between devices: 7.6 us -> 19.5 us  [shards(): lax.psum(down_key.astype(jnp.bfloat16), 'dp').astype(jnp.float32)]
  transfers between devices with their start and end apart: 6 -> 6, of which waited for: 6 -> 6; matrix products, arithmetic and copies ran while one was open for 13% -> 6% of each run, Pallas kernels for 0% -> 0%
where the time goes in v1:
time: 500 us; the launch traced here: 499 us
  waiting for transfers between devices  291 us (58%)
  Pallas kernels  148 us (30%)
  matrix products  24.2 us (5%)
  between operations  14.2 us (3%)
  blocking collectives  12 us (2%)
    pallas_call x1, Pallas kernels, attention_grads(): pl.pallas_call(functools.partial(attention_kernel, n, heads, lag), grid=(...  148 us
    psum x1, waiting for transfers between devices, shards(): lax.psum(up_key.astype(jnp.bfloat16), ('dp', 'seq')).astype(jnp.float32)  113 us
    reduce_scatter x1, waiting for transfers between devices, shards(): lax.psum_scatter(contract_last(grad_text, out_weight).astype(jnp.bfloat16...  93.7 us
    psum x1, waiting for transfers between devices, shards(): latent = lax.psum(latent_part.astype(jnp.bfloat16), 'seq')  32.8 us
    psum x1, waiting for transfers between devices, shards(): lax.psum(down_key.astype(jnp.bfloat16), 'dp').astype(jnp.float32)  19.5 us
    psum x1, waiting for transfers between devices, shards(): lax.psum(context_part, 'tp').astype(jnp.float32)  17.4 us
    dot_general x3, matrix products, contract_last(): lax.dot_general(left_side, right_side, (((1,), (1,)), ((), ())), preferre...  15.6 us
    psum x1, waiting for transfers between devices, shards(): lax.psum(key_project, 'tp').astype(jnp.float32)  14.5 us
  transfers between devices with their start and end apart: 6, of which 6 were waited for; matrix products, arithmetic and copies ran while one was open for 6% of the time, Pallas kernels for 0%

profile of v1, /device:TPU:0, one launch (start us, length us, event | category | flops | bytes accessed | tf_op | source)
XLA Modules:
  0.0 499.2 jit_solution(7483668072043992503)
XLA Ops:
  7.2 0.0 copy-start
  7.2 0.0 all-reduce.17.cloned.1.call-start
  7.2 0.0 copy-start.1
  7.2 0.9 copy-done.1
  8.2 0.9 copy-done.2
  9.1 148.3 %attention.1 = (bf16[512,2560]{1,0:T(8,128)(2,1)}, bf16[512,2560]{1,0:T(8,128)(2,1)}, bf16[512,2560]{1,0:T(8,128)(2,1)}, bf16[512,1024]{1,0:T(8,128)(2,1)}, bf16...) custom-call(bf16[512,2560]{1,0:T(8,128)(2,1)} %bitcast.30, bf16[512,2560]{1,0:T(8,128)(2,1)} %bitcast.31, ...), custom_call_target="tpu_custom_call" | custom-call | flops 9395240960 | bytes 15728640 | tf_op jit(solution)/shard_map/attention/pallas_call | solution.py:220
  157.4 0.0 all-reduce.17.cloned.1.call-update
  157.4 0.0 all-reduce.11.cloned.1.call-start
  157.4 0.0 copy-done.3
  157.5 0.0 copy-done.8
  157.5 0.0 copy-done.9
  157.5 0.4 convolution_convert_fusion.6
  157.9 0.0 copy-done
  157.9 0.4 convolution_convert_fusion.5
  158.3 0.7 pad_maximum_fusion
  159.0 0.0 all-reduce.11.cloned.1.call-update
  159.0 0.0 all-reduce.9.cloned.1.call-start
  159.1 0.7 all-reduce.9.cloned.1.call-update
  159.7 0.0 all-reduce.15.cloned.1.call-start
  159.8 14.5 %all-reduce.17.cloned.1.call-done = (bf16[512,32]{1,0:T(8,128)(2,1)}, bf16[512,32]{1,0:T(8,128)(2,1)}) async-done(((bf16[512,32]{1,0:T(8,128)(2,1)}, bf16[512,32]{1,0:T(8,128)(2,1)}), (bf16[512,32]{1,0:T(8,128)(2,1)}, bf16[512,32]{1,0:T(8,128)(2,1)})) %all-reduce.17.cloned.1.call-update) | async-done | bytes 65552 | tf_op jit(solution)/shard_map/psum | solution.py:320
  174.3 1.9 convolution_convert_fusion.4
  176.2 1.9 convolution_convert_fusion.3
  178.1 0.0 copy-done.6
  178.1 1.7 fusion.15
  179.8 0.0 all-reduce.15.cloned.1.call-update
  179.8 0.0 all-reduce.13.cloned.1.call-start
  179.9 32.8 %all-reduce.11.cloned.1.call-done = bf16[512,64]{0,1:T(8,128)(2,1)} async-done(((bf16[512,64]{0,1:T(8,128)(2,1)}), bf16[512,64]{0,1:T(8,128)(2,1)}) %all-reduce.11.cloned.1.call-update) | async-done | bytes 65552 | tf_op jit(solution)/shard_map/psum | solution.py:307
  212.7 2.0 convolution_convert_fusion.2
  214.7 2.0 convolution_convert_fusion.1
  216.7 0.0 all-reduce.13.cloned.1.call-update
  216.7 0.0 copy-start.10
  216.7 0.0 reduce-scatter.2.cloned.1.call-start
  216.8 17.4 %all-reduce.9.cloned.1.call-done = bf16[512,1024]{1,0:T(8,128)(2,1)} async-done(((bf16[512,1024]{1,0:T(8,128)(2,1)}), bf16[512,1024]{1,0:T(8,128)(2,1)}) %all-reduce.9.cloned.1.call-update) | async-done | bytes 1048592 | tf_op jit(solution)/shard_map/psum | solution.py:319
  234.2 0.0 copy-done.7
  234.2 2.5 fusion
  236.7 12.0 %psum.66 = f32[512]{0:T(512)S(1)} all-reduce(f32[512]{0:T(512)S(1)} %get-tuple-element.25), channel_id=1, replica_groups=mesh['dp'=4,'seq'=4,'tp'=2] {'seq'}, use_global_device_ids=true, to_apply=%region_4.0 | all-reduce | flops 512 | bytes 4096 | tf_op jit(solution)/shard_map/psum | solution.py:277
  248.7 0.4 fusion.3
  249.1 0.0 copy-start.5
  249.1 1.0 copy-done.5
  250.0 11.4 %convolution_convert_fusion = bf16[512,5120]{1,0:T(8,128)(2,1)} fusion(bf16[512,1024]{1,0:T(8,128)(2,1)S(1)} %fusion.3, bf16[5120,1024]{1,0:T(8,128)(2,1)} %param.27), kind=kOutput, calls=%fused_computation | convolution fusion | flops 5371330560 | bytes 16777216 | tf_op jit(solution)/shard_map/dot_general | solution.py:16
  261.4 0.0 reduce-scatter.2.cloned.1.call-update
  261.4 19.5 %all-reduce.15.cloned.1.call-done = (bf16[1024,32]{0,1:T(8,128)(2,1)}, bf16[1024,32]{0,1:T(8,128)(2,1)}) async-done(((bf16[1024,32]{0,1:T(8,128)(2,1)}, bf16[1024,32]{0,1:T(8,128)(2,1)}), (bf16[1024,32]{0,1:T(8,128)(2,1)}, bf16[1024,32]{0,1:T(8,128)(2,1)})) %all-reduce.15.cloned.1.call-update) | async-done | bytes 131088 | tf_op jit(solution)/shard_map/psum | solution.py:349
  280.9 1.6 convert_multiply_fusion.5
  282.5 112.7 %all-reduce.13.cloned.1.call-done = (bf16[32,2560]{1,0:T(8,128)(2,1)}, bf16[32,2560]{1,0:T(8,128)(2,1)}) async-done(((bf16[32,2560]{1,0:T(8,128)(2,1)}, bf16[32,2560]{1,0:T(8,128)(2,1)}), (bf16[32,2560]{1,0:T(8,128)(2,1)}, bf16[32,2560]{1,0:T(8,128)(2,1)})) %all-reduce.13.cloned.1.call-update) | async-done | bytes 327696 | tf_op jit(solution)/shard_map/psum | solution.py:353
  395.2 1.9 convert_multiply_fusion.3
  397.1 93.7 %reduce-scatter.2.cloned.1.call-done = bf16[128,5120]{1,0:T(8,128)(2,1)} async-done(((bf16[512,5120]{1,0:T(8,128)(2,1)}), bf16[128,5120]{1,0:T(8,128)(2,1)}) %reduce-scatter.2.cloned.1.call-update) | async-done | bytes 1310736 | tf_op jit(solution)/shard_map/reduce_scatter | solution.py:356
  490.8 0.0 copy-done.4
  490.8 1.5 copy.30
  (9 shorter events, 0.0 us)
Async XLA Ops:
  7.2 150.7 %copy-start = (bf16[1024,32]{0,1:T(8,128)(2,1)S(1)}, bf16[1024,32]{0,1:T(8,128)(2,1)}, u32[]{:S(2)}) copy-start(bf16[1024,32]{0,1:T(8,128)(2,1)} %param.25) | copy-start | bytes 196612
  7.2 167.1 %all-reduce.17.cloned.1.call-start = ((), (), s32[]{:S(2)}) async-start(), calls=%async_computation.6 | async-start | bytes 524288 | tf_op jit(solution)/shard_map/psum | solution.py:320
  7.2 0.9 copy-start.1
  8.1 0.9 copy-start.2
  9.1 148.4 %copy-start.3 = (bf16[1,512,1024]{2,1,0:T(8,128)(2,1)S(1)}, bf16[1,512,1024]{2,1,0:T(8,128)(2,1)}, u32[]{:S(2)}) copy-start(bf16[1,512,1024]{2,1,0:T(8,128)(2,1)} %param.18) | copy-start | bytes 3145732
  9.1 148.4 %copy-start.8 = (bf16[1024,32]{0,1:T(8,128)(2,1)S(1)}, bf16[1024,32]{0,1:T(8,128)(2,1)}, u32[]{:S(2)}) copy-start(bf16[1024,32]{0,1:T(8,128)(2,1)} %param.23) | copy-start | bytes 196612
  9.1 148.4 %copy-start.9 = (f32[1024]{0:T(1024)S(1)}, f32[1024]{0:T(1024)}, u32[]{:S(2)}) copy-start(f32[1024]{0:T(1024)} %param.20) | copy-start | bytes 12292
  157.4 55.3 %all-reduce.11.cloned.1.call-start = ((), (), s32[]{:S(2)}) async-start(), calls=%async_computation.3 | async-start | bytes 131072 | tf_op jit(solution)/shard_map/psum | solution.py:307
  159.0 75.1 %all-reduce.9.cloned.1.call-start = ((), (), s32[]{:S(2)}) async-start(), calls=%async_computation.1 | async-start | bytes 2097152 | tf_op jit(solution)/shard_map/psum | solution.py:319
  159.7 121.2 %all-reduce.15.cloned.1.call-start = ((), (), s32[]{:S(2)}) async-start(), calls=%async_computation.5 | async-start | bytes 262144 | tf_op jit(solution)/shard_map/psum | solution.py:349
  174.2 3.8 copy-start.6
  178.1 56.1 %copy-start.7 = (bf16[512,32]{1,0:T(8,128)(2,1)S(1)}, bf16[512,32]{1,0:T(8,128)(2,1)}, u32[]{:S(2)}) copy-start(bf16[512,32]{1,0:T(8,128)(2,1)} %get-tuple-element.24) | copy-start | bytes 98308
  179.8 215.4 %all-reduce.13.cloned.1.call-start = ((), (), s32[]{:S(2)}) async-start(), calls=%async_computation.4 | async-start | bytes 655360 | tf_op jit(solution)/shard_map/psum | solution.py:353
  216.7 32.0 %copy-start.10 = (f32[1,512]{1,0:T(1,128)S(1)}, f32[1,512]{1,0:T(1,128)}, u32[]{:S(2)}) copy-start(f32[1,512]{1,0:T(1,128)} %param.19) | copy-start | bytes 6148
  216.7 274.1 %reduce-scatter.2.cloned.1.call-start = ((), (), s32[]{:S(2)}) async-start(), calls=%async_computation.2 | async-start | bytes 6553600 | tf_op jit(solution)/shard_map/reduce_scatter | solution.py:356
  249.1 1.0 copy-start.5
  261.4 229.5 %copy-start.4 = (bf16[512,2560]{1,0:T(8,128)(2,1)S(1)}, bf16[512,2560]{1,0:T(8,128)(2,1)}, u32[]{:S(2)}) copy-start(bf16[512,2560]{1,0:T(8,128)(2,1)} %get-tuple-element.13) | copy-start | bytes 7864324
Sparse Core Ops, SparseCore 0:
  157.5 16.6 all-reduce.16
  177.1 35.4 all-reduce.10
  215.0 19.0 all-reduce.8
  237.5 43.4 all-reduce.14
  286.6 108.6 all-reduce.12
  398.0 92.8 reduce-scatter.1

commit v2 on v1

--- a/solution.py
+++ b/solution.py
@@ -8,20 +8,7 @@
 from jax.sharding import PartitionSpec as P
 
 HD = 128
-DT = 4096
 MESH = pl.DeviceIdType.MESH
-
-
-def contract_last(left_side, right_side):
-    return lax.dot_general(
-        left_side, right_side, (((1,), (1,)), ((), ())), preferred_element_type=jnp.float32
-    )
-
-
-def contract_first(left_side, right_side):
-    return lax.dot_general(
-        left_side, right_side, (((0,), (0,)), ((), ())), preferred_element_type=jnp.float32
-    )
 
 
 def dot(left_side, right_side, left_dim, right_dim):
@@ -49,8 +36,7 @@
     key_grad,
     value_grad,
     context,
-    key_project,
-    value_project,
+    project,
     part,
     up_in,
     up_out,
@@ -191,8 +177,9 @@
     @pl.when(step == heads + lag - 1)
     def _():
         context[...] = total[...].astype(jnp.bfloat16)
-        key_project[...] = key_total[...].astype(jnp.bfloat16)
-        value_project[...] = value_total[...].astype(jnp.bfloat16)
+        project[...] = jnp.concatenate([key_total[...], value_total[...]], axis=1).astype(
+            jnp.bfloat16
+        )
 
 
 def attention_grads(
@@ -225,8 +212,7 @@
             jax.ShapeDtypeStruct((length, columns), jnp.bfloat16),
             jax.ShapeDtypeStruct((length, columns), jnp.bfloat16),
             jax.ShapeDtypeStruct((length, features), jnp.bfloat16),
-            jax.ShapeDtypeStruct((length, rank), jnp.bfloat16),
-            jax.ShapeDtypeStruct((length, rank), jnp.bfloat16),
+            jax.ShapeDtypeStruct((length, 2 * rank), jnp.bfloat16),
         ),
         in_specs=[
             early(rows),
@@ -243,8 +229,7 @@
             late(length),
             late(length),
             fixed(length, features),
-            fixed(length, rank),
-            fixed(length, rank),
+            fixed(length, 2 * rank),
         ),
         scratch_shapes=[buffer] * 5
         + [
@@ -265,18 +250,378 @@
     )(queries, keys, values, grad_attention, key_weight, value_weight, key_up, value_up)
 
 
-def norm_backward(
-    context_base, key_back, value_back, text_rows, scale_rows, norm_gain, key_down, value_down
+def exchange(axis, size, source, landing, send, recv):
+    me = lax.axis_index(axis)
+
+    def copy(offset):
+        return pltpu.make_async_remote_copy(
+            src_ref=source,
+            dst_ref=landing.at[me],
+            send_sem=send.at[offset],
+            recv_sem=recv.at[me],
+            device_id={axis: lax.rem(me + offset, size)},
+            device_id_type=MESH,
+        )
+
+    def arrival(offset):
+        other = lax.rem(me + offset, size)
+        return pltpu.make_async_remote_copy(
+            src_ref=source,
+            dst_ref=landing.at[other],
+            send_sem=send.at[offset],
+            recv_sem=recv.at[other],
+            device_id={axis: other},
+            device_id_type=MESH,
+        )
+
+    def start():
+        for offset in range(1, size):
+            copy(offset).start()
+
+    def finish():
+        for offset in range(1, size):
+            arrival(offset).wait_recv()
+        for offset in range(1, size):
+            copy(offset).wait_send()
+
+    return start, finish
+
+
+def tail_kernel(
+    n,
+    splits,
+    prompts,
+    slices,
+    features_whole,
+    context_part,
+    project_part,
+    normed,
+    scale,
+    gain,
+    down,
+    latent,
+    key_grad,
+    value_grad,
+    out_weight,
+    grad_text,
+    grad_hidden,
+    down_sum,
+    up_sum,
+    weight,
+    grads,
+    context_all,
+    project_all,
+    scaled,
+    sum_own,
+    sum_all,
+    up_own,
+    up_all,
+    down_own,
+    down_all,
+    rows_own,
+    rows_all,
+    part,
+    up_in,
+    up_out,
+    down_in,
+    down_out,
+    weight_sem,
+    grads_sem,
+    context_send,
+    context_recv,
+    project_send,
+    project_recv,
+    sum_send,
+    sum_recv,
+    up_dp_send,
+    up_dp_recv,
+    down_dp_send,
+    down_dp_recv,
+    rows_send,
+    rows_recv,
+    high_send,
+    high_recv,
+    low_send,
+    low_recv,
 ):
-    grad_context = (
-        context_base + contract_last(key_back, key_down) + contract_last(value_back, value_down)
-    )
-    text_values = text_rows.astype(jnp.float32)
-    scaled = norm_gain * grad_context
-    local_sum = jnp.sum(text_values * scaled, axis=1)
-    token_sum = lax.psum(local_sum, "seq")
-    return (scale_rows[:, None] * (scaled - text_values * (token_sum / DT)[:, None])).astype(
-        jnp.bfloat16
+    me = lax.axis_index("seq")
+    split = lax.axis_index("tp")
+    prompt = lax.axis_index("dp")
+    length = grad_text.shape[0]
+    width = part.shape[3]
+    block = part.shape[2]
+    lag = n
+    has_low = me > 0
+    has_high = me < n - 1
+
+    key_fetch = pltpu.make_async_copy(key_grad, grads, grads_sem)
+    value_fetch = pltpu.make_async_copy(value_grad, grads, grads_sem)
+    weight_fetch = pltpu.make_async_copy(out_weight, weight, weight_sem)
+
+    @pl.when(me < n // 2)
+    def _():
+        key_fetch.start()
+
+    @pl.when(me >= n // 2)
+    def _():
+        value_fetch.start()
+
+    weight_fetch.start()
+
+    barrier = pltpu.get_barrier_semaphore()
+    for axis, size in (("tp", splits), ("seq", n), ("dp", prompts)):
+        for offset in range(1, size):
+            pl.semaphore_signal(
+                barrier,
+                inc=1,
+                device_id={axis: lax.rem(lax.axis_index(axis) + offset, size)},
+                device_id_type=MESH,
+            )
+    pl.semaphore_wait(barrier, splits + n + prompts - 3)
+
+    project_start, project_finish = exchange(
+        "tp", splits, project_part, project_all, project_send, project_recv
+    )
+    context_start, context_finish = exchange(
+        "tp", splits, context_part, context_all, context_send, context_recv
+    )
+    sum_start, sum_finish = exchange("seq", n, sum_own, sum_all, sum_send, sum_recv)
+    up_start, up_finish = exchange("dp", prompts, up_own, up_all, up_dp_send, up_dp_recv)
+    down_start, down_finish = exchange(
+        "dp", prompts, down_own, down_all, down_dp_send, down_dp_recv
+    )
+    rows_start, rows_finish = exchange("seq", n, rows_own, rows_all, rows_send, rows_recv)
+
+    project_start()
+    context_start()
+    project_all[split] = project_part[...]
+    context_all[split] = context_part[...]
+    key_fetch.wait()
+    up_own[...] = dot(latent[...], grads[...], 1, 0).astype(jnp.bfloat16)
+    up_all[prompt] = up_own[...]
+    up_start()
+
+    project_finish()
+    back = project_all[0].astype(jnp.float32)
+    for index in range(1, splits):
+        back = back + project_all[index].astype(jnp.float32)
+    back = back.astype(jnp.bfloat16)
+    low_rank = dot(back, down[...], 1, 1)
+    context_finish()
+    whole = context_all[0].astype(jnp.float32)
+    for index in range(1, splits):
+        whole = whole + context_all[index].astype(jnp.float32)
+    scaled[...] = gain[...] * (whole + low_rank)
+    local_sum = jnp.sum(normed[...].astype(jnp.float32) * scaled[...], axis=1, keepdims=True)
+    sum_own[...] = jnp.transpose(jnp.broadcast_to(local_sum, (length, 128)))[:8, :]
+    sum_all[me] = sum_own[...]
+    sum_start()
+
+    context = (normed[...].astype(jnp.float32) * gain[...]).astype(jnp.bfloat16)
+    down_own[...] = dot(back, context, 0, 0).astype(jnp.bfloat16)
+    down_all[prompt] = down_own[...]
+    down_start()
+    weight_fetch.wait()
+
+    sum_finish()
+    token_sum = sum_all[0]
+    for index in range(1, n):
+        token_sum = token_sum + sum_all[index]
+    token_column = jnp.transpose(jnp.broadcast_to(token_sum[:1, :], (128, length)))[:, :1]
+    grad_text[...] = (
+        scale[...]
+        * (scaled[...] - normed[...].astype(jnp.float32) * (token_column / features_whole))
+    ).astype(jnp.bfloat16)
+
+    def high_copy(chunk, owner, source):
+        return pltpu.make_async_remote_copy(
+            src_ref=source.at[chunk, owner],
+            dst_ref=up_in.at[chunk, owner],
+            send_sem=high_send.at[chunk, owner],
+            recv_sem=high_recv.at[chunk, owner],
+            device_id={"seq": lax.rem(me + 1, n)},
+            device_id_type=MESH,
+        )
+
+    def low_copy(chunk, owner, source):
+        return pltpu.make_async_remote_copy(
+            src_ref=source.at[chunk, owner],
+            dst_ref=down_in.at[chunk, owner],
+            send_sem=low_send.at[chunk, owner],
+            recv_sem=low_recv.at[chunk, owner],
+            device_id={"seq": lax.rem(me + n - 1, n)},
+            device_id_type=MESH,
+        )
+
+    def hidden_step(step, carry):
+        @pl.when(step < slices)
+        def _():
+            slab = weight[pl.ds(pl.multiple_of(step * width, width), width), :]
+            product = dot(grad_text[...], slab, 1, 1).astype(jnp.bfloat16)
+            part[step] = product.reshape(n, block, width)
+
+        high = step - me
+        high_live = jnp.logical_and(high >= 0, high < slices)
+
+        @pl.when(jnp.logical_and(high_live, me == 0))
+        def _():
+            def send(index, carry):
+                high_copy(high, n - 1 - index, part).start()
+                return carry
+
+            lax.fori_loop(0, n - 1, send, 0)
+            up_in[high, 0] = jnp.zeros(up_in.shape[2:], up_in.dtype)
+
+        @pl.when(jnp.logical_and(high_live, has_low))
+        def _():
+            def forward(index, carry):
+                owner = n - 1 - index
+                high_copy(high, owner, up_out).wait_recv()
+                up_out[high, owner] = up_in[high, owner] + part[high, owner]
+                high_copy(high, owner, up_out).start()
+                return carry
+
+            lax.fori_loop(0, n - 1 - me, forward, 0)
+            high_copy(high, me, up_out).wait_recv()
+
+        low = step - (n - 1 - me)
+        low_live = jnp.logical_and(low >= 0, low < slices)
+
+        @pl.when(jnp.logical_and(low_live, me == n - 1))
+        def _():
+            def send(owner, carry):
+                low_copy(low, owner, part).start()
+                return carry
+
+            lax.fori_loop(0, n - 1, send, 0)
+            down_in[low, n - 1] = jnp.zeros(down_in.shape[2:], down_in.dtype)
+
+        @pl.when(jnp.logical_and(low_live, has_high))
+        def _():
+            def forward(owner, carry):
+                low_copy(low, owner, down_out).wait_recv()
+                down_out[low, owner] = down_in[low, owner] + part[low, owner]
+                low_copy(low, owner, down_out).start()
+                return carry
+
+            lax.fori_loop(0, me, forward, 0)
+            low_copy(low, me, down_out).wait_recv()
+
+        @pl.when(step >= lag)
+        def _():
+            chunk = step - lag
+
+            def high_done(owner, carry):
+                high_copy(chunk, owner, up_out).wait_send()
+                return carry
+
+            def low_done(owner, carry):
+                low_copy(chunk, owner, down_out).wait_send()
+                return carry
+
+            lax.fori_loop(me + 1, n, high_done, 0)
+            lax.fori_loop(0, me, low_done, 0)
+            grad_hidden[:, pl.ds(pl.multiple_of(chunk * width, width), width)] = (
+                up_in[chunk, me].astype(jnp.float32)
+                + part[chunk, me].astype(jnp.float32)
+                + down_in[chunk, me].astype(jnp.float32)
+            ).astype(jnp.bfloat16)
+
+        return carry
+
+    lax.fori_loop(0, slices // 2, hidden_step, 0)
+
+    up_finish()
+    up_total = up_all[0].astype(jnp.float32)
+    for index in range(1, prompts):
+        up_total = up_total + up_all[index].astype(jnp.float32)
+    rows_own[...] = (up_total / prompts).astype(jnp.bfloat16)
+    rows_all[me] = rows_own[...]
+    rows_start()
+    down_finish()
+    down_total = down_all[0].astype(jnp.float32)
+    for index in range(1, prompts):
+        down_total = down_total + down_all[index].astype(jnp.float32)
+    down_sum[...] = down_total / prompts
+
+    lax.fori_loop(slices // 2, slices + lag, hidden_step, 0)
+    rows_finish()
+    up_sum[...] = rows_all[...].astype(jnp.float32)
+
+
+def tail(
+    context_part,
+    project_part,
+    normed,
+    scale,
+    gain,
+    down,
+    latent,
+    key_grad,
+    value_grad,
+    out_weight,
+):
+    length, features = context_part.shape
+    pair = project_part.shape[1]
+    columns = key_grad.shape[1]
+    hidden = out_weight.shape[0]
+    n, splits, prompts = lax.axis_size("seq"), lax.axis_size("tp"), lax.axis_size("dp")
+    width = 512 if hidden % 512 == 0 else 256
+    slices = hidden // width
+    block = length // n
+    share = pair // n
+    low = jnp.bfloat16
+    buffer = pltpu.VMEM((slices, n, block, width), low)
+    dma = pltpu.SemaphoreType.DMA
+    vmem = pl.BlockSpec(memory_space=pltpu.VMEM)
+    hbm = pl.BlockSpec(memory_space=pl.ANY)
+    return pl.pallas_call(
+        functools.partial(tail_kernel, n, splits, prompts, slices, features * n),
+        out_shape=(
+            jax.ShapeDtypeStruct((length, features), low),
+            jax.ShapeDtypeStruct((block, hidden), low),
+            jax.ShapeDtypeStruct((pair, features), jnp.float32),
+            jax.ShapeDtypeStruct((n, share, columns), jnp.float32),
+        ),
+        in_specs=[vmem] * 7 + [hbm] * 3,
+        out_specs=(vmem,) * 4,
+        scratch_shapes=[
+            pltpu.VMEM(out_weight.shape, low),
+            pltpu.VMEM(key_grad.shape, low),
+            pltpu.VMEM((splits, length, features), low),
+            pltpu.VMEM((splits, length, pair), low),
+            pltpu.VMEM((length, features), jnp.float32),
+            pltpu.VMEM((8, length), jnp.float32),
+            pltpu.VMEM((n, 8, length), jnp.float32),
+            pltpu.VMEM((share, columns), low),
+            pltpu.VMEM((prompts, share, columns), low),
+            pltpu.VMEM((pair, features), low),
+            pltpu.VMEM((prompts, pair, features), low),
+            pltpu.VMEM((share, columns), low),
+            pltpu.VMEM((n, share, columns), low),
+        ]
+        + [buffer] * 5
+        + [dma, dma]
+        + [dma((splits,))] * 4
+        + [dma((n,))] * 2
+        + [dma((prompts,))] * 4
+        + [dma((n,))] * 2
+        + [dma((slices, n))] * 4,
+        compiler_params=pltpu.CompilerParams(
+            collective_id=1, has_side_effects=True, vmem_limit_bytes=60 * 1024 * 1024
+        ),
+        name="tail",
+    )(
+        context_part,
+        project_part,
+        normed,
+        scale,
+        gain,
+        down,
+        latent,
+        key_grad,
+        value_grad,
+        out_weight,
     )
 
 
@@ -305,7 +650,10 @@
         axis=1,
     )
     latent = lax.psum(latent_part.astype(jnp.bfloat16), "seq")
-    grad_query, key_grad, value_grad, context_part, key_project, value_project = attention_grads(
+    n = lax.axis_size("seq")
+    rank = key_down.shape[1]
+    share = 2 * rank // n
+    grad_query, key_grad, value_grad, context_part, project_part = attention_grads(
         queries[0],
         keys[0],
         values[0],
@@ -315,58 +663,28 @@
         key_up,
         value_up,
     )
-    context_base, key_total, value_total = (
-        lax.psum(context_part, "tp").astype(jnp.float32),
-        lax.psum(key_project, "tp").astype(jnp.float32),
-        lax.psum(value_project, "tp").astype(jnp.float32),
-    )
-    key_back = key_total.astype(jnp.bfloat16)
-    value_back = value_total.astype(jnp.bfloat16)
-    grad_text = norm_backward(
-        context_base,
-        key_back,
-        value_back,
+    latent_rows = lax.dynamic_slice_in_dim(latent.T, lax.axis_index("seq") * share, share, 0)
+    grad_text, grad_hidden, down_sum, up_sum = tail(
+        context_part,
+        project_part,
         normed[0],
-        norm_scale[0],
-        norm_gain,
-        key_down,
-        value_down,
-    )
-    prompt_count = lax.axis_size("dp")
-    down_key = contract_first(context, key_back)
-    down_value = contract_first(context, value_back)
-    rank = key_down.shape[1]
-    block = key_grad.shape[0] // lax.axis_size("seq")
-    start = lax.axis_index("seq") * block
-    latent_block = lax.dynamic_slice_in_dim(latent, start, block, 0)
-    up_key = contract_first(
-        latent_block[:, :rank], lax.dynamic_slice_in_dim(key_grad, start, block, 0)
-    )
-    up_value = contract_first(
-        latent_block[:, rank:], lax.dynamic_slice_in_dim(value_grad, start, block, 0)
-    )
-    down_key, down_value = (
-        lax.psum(down_key.astype(jnp.bfloat16), "dp").astype(jnp.float32),
-        lax.psum(down_value.astype(jnp.bfloat16), "dp").astype(jnp.float32),
-    )
-    up_key, up_value = (
-        lax.psum(up_key.astype(jnp.bfloat16), ("dp", "seq")).astype(jnp.float32),
-        lax.psum(up_value.astype(jnp.bfloat16), ("dp", "seq")).astype(jnp.float32),
-    )
-    grad_hidden = lax.psum_scatter(
-        contract_last(grad_text, out_weight).astype(jnp.bfloat16),
-        "seq",
-        scatter_dimension=0,
-        tiled=True,
-    )
+        norm_scale[0][:, None],
+        norm_gain[None, :],
+        jnp.concatenate([key_down, value_down], axis=1),
+        latent_rows,
+        key_grad,
+        value_grad,
+        out_weight,
+    )
+    up_rows = up_sum.reshape(2 * rank, up_sum.shape[2])
     return (
         grad_query[None],
         grad_text[None],
         grad_hidden[None],
-        down_key / prompt_count,
-        up_key / prompt_count,
-        down_value / prompt_count,
-        up_value / prompt_count,
+        down_sum[:rank].T,
+        up_rows[:rank],
+        down_sum[rank:].T,
+        up_rows[rank:],
     )
 
 

time: 500 us -> 294 us (0.59)
  waiting for transfers between devices: 291 us -> 0.02 us
  Pallas kernels: 148 us -> 263 us
  matrix products: 24.2 us -> 3.42 us
  blocking collectives: 12 us -> 0 us
  local copies, waits for them, and re-layouts: 4.33 us -> 11.8 us
    psum x4 -> x0, waiting for transfers between devices: 164 us -> none  [the longest x1 113 us: shards(): lax.psum(up_key.astype(jnp.bfloat16), ('dp', 'seq')).astype(jnp.float32)]
    pallas_call x0 -> x1, Pallas kernels: none -> 113 us  [tail(): pl.pallas_call(functools.partial(tail_kernel, n, splits, prompts, slices,...]
    reduce_scatter x1 -> x0, waiting for transfers between devices: 93.7 us -> none  [shards(): lax.psum_scatter(contract_last(grad_text, out_weight).astype(jnp.bfloat16...]
    psum x1, waiting for transfers between devices: 32.8 us -> 0.01 us  [shards(): latent = lax.psum(latent_part.astype(jnp.bfloat16), 'seq')]
    dot_general x7 -> x0, matrix products: 23.4 us -> none  [the longest x3 15.6 us: contract_last(): lax.dot_general(left_side, right_side, (((1,), (1,)), ((), ())), preferre...]
    psum x1 -> x0, blocking collectives: 12 us -> none  [norm_backward(): token_sum = lax.psum(local_sum, 'seq')]
  transfers between devices with their start and end apart: 6 -> 1, of which waited for: 6 -> 0; matrix products, arithmetic and copies ran while one was open for 6% -> 1% of each run, Pallas kernels for 0% -> 51%
where the time goes in v2:
time: 294 us
  Pallas kernels  263 us (89%)
  between operations  14.1 us (5%)
  local copies, waits for them, and re-layouts  11.8 us (4%)
  matrix products  3.42 us (1%)
    pallas_call x1, Pallas kernels, attention_grads(): pl.pallas_call(functools.partial(attention_kernel, n, heads, lag), grid=(...  150 us
    pallas_call x1, Pallas kernels, tail(): pl.pallas_call(functools.partial(tail_kernel, n, splits, prompts, slices,...  113 us
    unnamed x23, local copies, waits for them, and re-layouts  5.96 us
  transfers between devices with their start and end apart: 1, of which 0 were waited for; matrix products, arithmetic and copies ran while one was open for 1% of the time, Pallas kernels for 51%

profile of v2, /device:TPU:0, one launch (start us, length us, event | category | flops | bytes accessed | tf_op | source)
XLA Modules:
  0.0 293.8 jit_solution(9277604983220828980)
XLA Ops:
  7.2 0.0 copy-start.6
  7.2 0.0 copy-start.7
  7.2 0.0 copy-start.8
  7.2 0.0 copy-start.3
  7.2 0.0 copy-start.2
  7.2 0.0 all-reduce.2.cloned.1.call-start
  7.3 1.8 convolution_convert_fusion.1
  9.0 1.7 convolution_convert_fusion
  10.7 0.7 pad_maximum_fusion.1
  11.3 0.0 all-reduce.2.cloned.1.call-update
  11.4 0.0 copy-done.6
  11.4 0.2 copy.23
  11.6 0.0 copy-done.7
  11.6 0.2 copy.24
  11.7 0.0 copy-done.8
  11.8 0.9 copy.25.scale
  12.6 0.0 copy-done.3
  12.6 0.0 copy-done.2
  12.6 150.3 %attention.1 = (bf16[512,2560]{1,0:T(8,128)(2,1)S(1)}, bf16[512,2560]{1,0:T(8,128)(2,1)}, bf16[512,2560]{1,0:T(8,128)(2,1)}, bf16[512,1024]{1,0:T(8,128)(2,1)S(1)}, bf16[512,64]{1,0:T(8,128)(2,1)S(1)}) custom-call(bf16[512,2560]{1,0:T(8,128)(2,1)} %bitcast.36, bf16[512,2560]{1,0:T(8,128)(2,1)} %bitcast.37, bf16[512,2560]{1,0:T(8,128)(2,1)} %bitcast.38, ...), custom_call_target="tpu_custom_call" | custom-call | flops 9395240960 | bytes 15728640 | tf_op jit(solution)/shard_map/attention/pallas_call | solution.py:207
  162.9 0.0 copy-start
  162.9 1.0 copy-done
  163.9 0.0 copy-start.1
  163.9 0.7 copy-done.1
  164.5 0.8 pad_maximum_fusion.down
  165.4 0.0 all-reduce.2.cloned.1.call-done
  165.4 1.3 dynamic-slice_bitcast_fusion.latent
  166.7 112.6 %tail.1 = (bf16[512,1024]{1,0:T(8,128)(2,1)}, bf16[128,5120]{1,0:T(8,128)(2,1)}, f32[64,1024]{1,0:T(8,128)}, f32[4,16,2560]{2,1,0:T(8,128)}) custom-call(bf16[512,1024]{1,0:T(8,128)(2,1)} %copy-done, bf16[512,64]{1,0:T(8,128)(2,1)} %copy-done.1, bf16[512,1024]{1,0:T(8,128)(2,1)} %bitcast.30, f32[512,1]{1,0:T(8,128)} %copy.25.scale, f32[1,1024]{1,0:T(1,128)} %bitcast.34, ...), custom_call_target="tpu_custom_call" | custom-call | tf_op jit(solution)/shard_map/tail/pallas_call | solution.py:578
  279.3 1.7 slice_bitcast_fusion
  281.0 1.9 fusion.2
  282.9 0.0 copy-start.5
  282.9 0.0 copy-start.4
  282.9 1.5 copy.30
  284.4 0.5 copy-done.5
  284.9 1.0 copy.31
  285.9 0.0 copy-done.4
  285.9 1.1 copy.32
Async XLA Ops:
  7.2 4.2 %copy-start.6 = (bf16[1024,32]{0,1:T(8,128)(2,1)S(1)}, bf16[1024,32]{0,1:T(8,128)(2,1)}, u32[]{:S(2)}) copy-start(bf16[1024,32]{0,1:T(8,128)(2,1)} %param.23) | copy-start | bytes 196612
  7.2 4.4 %copy-start.7 = (bf16[1024,32]{0,1:T(8,128)(2,1)S(1)}, bf16[1024,32]{0,1:T(8,128)(2,1)}, u32[]{:S(2)}) copy-start(bf16[1024,32]{0,1:T(8,128)(2,1)} %param.25) | copy-start | bytes 196612
  7.2 4.6 %copy-start.8 = (f32[1,512]{1,0:T(1,128)S(1)}, f32[1,512]{1,0:T(1,128)}, u32[]{:S(2)}) copy-start(f32[1,512]{1,0:T(1,128)} %param.19) | copy-start | bytes 6148
  7.2 5.4 %copy-start.3 = (bf16[32,2560]{1,0:T(8,128)(2,1)S(1)}, bf16[32,2560]{1,0:T(8,128)(2,1)}, u32[]{:S(2)}) copy-start(bf16[32,2560]{1,0:T(8,128)(2,1)} %value_up.1) | copy-start | bytes 491524
  7.2 5.4 %copy-start.2 = (bf16[32,2560]{1,0:T(8,128)(2,1)S(1)}, bf16[32,2560]{1,0:T(8,128)(2,1)}, u32[]{:S(2)}) copy-start(bf16[32,2560]{1,0:T(8,128)(2,1)} %key_up.1) | copy-start | bytes 491524
  7.2 158.2 %all-reduce.2.cloned.1.call-start = ((), (), s32[]{:S(2)}) async-start(), calls=%async_computation | async-start | bytes 131072 | tf_op jit(solution)/shard_map/psum | solution.py:652
  162.9 1.0 copy-start
  163.9 0.7 copy-start.1
  282.9 2.0 copy-start.5
  282.9 2.9 copy-start.4
Sparse Core Ops, SparseCore 0:
  11.5 37.2 all-reduce.1

commit v3 on v2

--- a/solution.py
+++ b/solution.py
@@ -56,22 +56,22 @@
     has_low = me > 0
     has_high = me < n - 1
 
-    def up_copy(chunk, source):
+    def up_copy(chunk, half, source):
         return pltpu.make_async_remote_copy(
-            src_ref=source.at[chunk],
-            dst_ref=up_in.at[chunk],
-            send_sem=up_send.at[chunk],
-            recv_sem=up_recv.at[chunk],
+            src_ref=source.at[chunk, half],
+            dst_ref=up_in.at[chunk, half],
+            send_sem=up_send.at[chunk, half],
+            recv_sem=up_recv.at[chunk, half],
             device_id={"seq": lax.rem(me + 1, n)},
             device_id_type=MESH,
         )
 
-    def down_copy(chunk, source):
+    def down_copy(chunk, half, source):
         return pltpu.make_async_remote_copy(
-            src_ref=source.at[chunk],
-            dst_ref=down_in.at[chunk],
-            send_sem=down_send.at[chunk],
-            recv_sem=down_recv.at[chunk],
+            src_ref=source.at[chunk, half],
+            dst_ref=down_in.at[chunk, half],
+            send_sem=down_send.at[chunk, half],
+            recv_sem=down_recv.at[chunk, half],
             device_id={"seq": lax.rem(me + n - 1, n)},
             device_id_type=MESH,
         )
@@ -107,48 +107,51 @@
         scores = dot(key, query, 1, 1) * factor
         weights = jnp.exp(scores - jnp.max(scores, axis=0, keepdims=True))
         probability = weights * (1.0 / jnp.sum(weights, axis=0, keepdims=True))
-        part[step, :, HD:] = dot(probability.astype(jnp.bfloat16), grad, 1, 0).astype(jnp.bfloat16)
+        part[step, 1] = dot(probability.astype(jnp.bfloat16), grad, 1, 0).astype(jnp.bfloat16)
         grad_probs = dot(value, grad, 1, 1)
         grad_scores = probability * (
             grad_probs - jnp.sum(probability * grad_probs, axis=0, keepdims=True)
         )
         grad_low = grad_scores.astype(jnp.bfloat16)
-        part[step, :, :HD] = (dot(grad_low, query, 1, 0) * factor).astype(jnp.bfloat16)
+        part[step, 0] = (dot(grad_low, query, 1, 0) * factor).astype(jnp.bfloat16)
         grad_query[...] = (dot(grad_low, key, 0, 0) * factor).astype(jnp.bfloat16)
 
     up_chunk = step - me
     up_live = jnp.logical_and(up_chunk >= 0, up_chunk < heads)
-
-    @pl.when(jnp.logical_and(up_live, has_low))
-    def _():
-        up_copy(up_chunk, up_out).wait_recv()
-
-        @pl.when(has_high)
-        def _():
-            up_out[up_chunk] = up_in[up_chunk] + part[up_chunk]
-            up_copy(up_chunk, up_out).start()
+    down_chunk = step - (n - 1 - me)
+    down_live = jnp.logical_and(down_chunk >= 0, down_chunk < heads)
 
     @pl.when(jnp.logical_and(up_live, me == 0))
     def _():
-        up_copy(up_chunk, part).start()
+        for half in (1, 0):
+            up_copy(up_chunk, half, part).start()
         up_in[up_chunk] = jnp.zeros(up_in.shape[1:], up_in.dtype)
-
-    down_chunk = step - (n - 1 - me)
-    down_live = jnp.logical_and(down_chunk >= 0, down_chunk < heads)
-
-    @pl.when(jnp.logical_and(down_live, has_high))
-    def _():
-        down_copy(down_chunk, down_out).wait_recv()
-
-        @pl.when(has_low)
-        def _():
-            down_out[down_chunk] = down_in[down_chunk] + part[down_chunk]
-            down_copy(down_chunk, down_out).start()
 
     @pl.when(jnp.logical_and(down_live, me == n - 1))
     def _():
-        down_copy(down_chunk, part).start()
+        for half in (1, 0):
+            down_copy(down_chunk, half, part).start()
         down_in[down_chunk] = jnp.zeros(down_in.shape[1:], down_in.dtype)
+
+    for half in (1, 0):
+
+        @pl.when(jnp.logical_and(up_live, has_low))
+        def _():
+            up_copy(up_chunk, half, up_out).wait_recv()
+
+            @pl.when(has_high)
+            def _():
+                up_out[up_chunk, half] = up_in[up_chunk, half] + part[up_chunk, half]
+                up_copy(up_chunk, half, up_out).start()
+
+        @pl.when(jnp.logical_and(down_live, has_high))
+        def _():
+            down_copy(down_chunk, half, down_out).wait_recv()
+
+            @pl.when(has_low)
+            def _():
+                down_out[down_chunk, half] = down_in[down_chunk, half] + part[down_chunk, half]
+                down_copy(down_chunk, half, down_out).start()
 
     @pl.when(step >= lag)
     def _():
@@ -156,23 +159,25 @@
 
         @pl.when(has_high)
         def _():
-            up_copy(chunk, up_out).wait_send()
+            for half in (1, 0):
+                up_copy(chunk, half, up_out).wait_send()
 
         @pl.when(has_low)
         def _():
-            down_copy(chunk, down_out).wait_send()
+            for half in (1, 0):
+                down_copy(chunk, half, down_out).wait_send()
 
         both = (
             up_in[chunk].astype(jnp.float32)
             + part[chunk].astype(jnp.float32)
             + down_in[chunk].astype(jnp.float32)
         ).astype(jnp.bfloat16)
-        key_grad[...] = both[:, :HD]
-        value_grad[...] = both[:, HD:]
+        key_grad[...] = both[0]
+        value_grad[...] = both[1]
         slab = jnp.concatenate([key_weight[...], value_weight[...]], axis=1)
-        total[...] += dot(both, slab, 1, 1)
-        key_total[...] += dot(both[:, :HD], key_up[...], 1, 1)
-        value_total[...] += dot(both[:, HD:], value_up[...], 1, 1)
+        total[...] += dot(jnp.concatenate([both[0], both[1]], axis=1), slab, 1, 1)
+        key_total[...] += dot(both[0], key_up[...], 1, 1)
+        value_total[...] += dot(both[1], value_up[...], 1, 1)
 
     @pl.when(step == heads + lag - 1)
     def _():
@@ -202,8 +207,8 @@
     def fixed(height, width):
         return pl.BlockSpec((height, width), lambda step: (0, 0))
 
-    buffer = pltpu.VMEM((heads, length, 2 * HD), jnp.bfloat16)
-    semaphores = pltpu.SemaphoreType.DMA((heads,))
+    buffer = pltpu.VMEM((heads, 2, length, HD), jnp.bfloat16)
+    semaphores = pltpu.SemaphoreType.DMA((heads, 2))
     return pl.pallas_call(
         functools.partial(attention_kernel, n, heads, lag),
         grid=(heads + lag,),
@@ -298,15 +303,17 @@
     normed,
     scale,
     gain,
-    down,
-    latent,
+    key_down,
+    value_down,
     key_grad,
     value_grad,
     out_weight,
     grad_text,
     grad_hidden,
-    down_sum,
-    up_sum,
+    key_down_grad,
+    value_down_grad,
+    key_up_grad,
+    value_up_grad,
     weight,
     grads,
     context_all,
@@ -320,6 +327,8 @@
     down_all,
     rows_own,
     rows_all,
+    latent_own,
+    latent_all,
     part,
     up_in,
     up_out,
@@ -339,6 +348,8 @@
     down_dp_recv,
     rows_send,
     rows_recv,
+    latent_send,
+    latent_recv,
     high_send,
     high_recv,
     low_send,
@@ -392,21 +403,50 @@
     )
     rows_start, rows_finish = exchange("seq", n, rows_own, rows_all, rows_send, rows_recv)
 
+    def latent_copy(offset):
+        other = lax.rem(me + offset, n)
+        return pltpu.make_async_remote_copy(
+            src_ref=latent_own.at[other],
+            dst_ref=latent_all.at[me],
+            send_sem=latent_send.at[offset],
+            recv_sem=latent_recv.at[me],
+            device_id={"seq": other},
+            device_id_type=MESH,
+        )
+
+    def latent_arrival(offset):
+        other = lax.rem(me + offset, n)
+        return pltpu.make_async_remote_copy(
+            src_ref=latent_own.at[other],
+            dst_ref=latent_all.at[other],
+            send_sem=latent_send.at[offset],
+            recv_sem=latent_recv.at[other],
+            device_id={"seq": other},
+            device_id_type=MESH,
+        )
+
     project_start()
     context_start()
     project_all[split] = project_part[...]
     context_all[split] = context_part[...]
-    key_fetch.wait()
-    up_own[...] = dot(latent[...], grads[...], 1, 0).astype(jnp.bfloat16)
-    up_all[prompt] = up_own[...]
-    up_start()
+    context = (normed[...].astype(jnp.float32) * gain[...]).astype(jnp.bfloat16)
+    latent_rows = jnp.concatenate(
+        [dot(key_down[...], context, 0, 1), dot(value_down[...], context, 0, 1)], axis=0
+    )
+    latent_own[...] = latent_rows.reshape(latent_own.shape).astype(jnp.bfloat16)
+    for offset in range(1, n):
+        latent_copy(offset).start()
+    latent_all[me] = latent_own[me]
 
     project_finish()
     back = project_all[0].astype(jnp.float32)
     for index in range(1, splits):
         back = back + project_all[index].astype(jnp.float32)
     back = back.astype(jnp.bfloat16)
-    low_rank = dot(back, down[...], 1, 1)
+    rank = key_down.shape[1]
+    low_rank = dot(back[:, :rank], key_down[...], 1, 1) + dot(
+        back[:, rank:], value_down[...], 1, 1
+    )
     context_finish()
     whole = context_all[0].astype(jnp.float32)
     for index in range(1, splits):
@@ -417,11 +457,21 @@
     sum_all[me] = sum_own[...]
     sum_start()
 
-    context = (normed[...].astype(jnp.float32) * gain[...]).astype(jnp.bfloat16)
     down_own[...] = dot(back, context, 0, 0).astype(jnp.bfloat16)
     down_all[prompt] = down_own[...]
     down_start()
+    for offset in range(1, n):
+        latent_arrival(offset).wait_recv()
+    latent = latent_all[0].astype(jnp.float32)
+    for index in range(1, n):
+        latent = latent + latent_all[index].astype(jnp.float32)
+    key_fetch.wait()
+    up_own[...] = dot(latent.astype(jnp.bfloat16), grads[...], 1, 0).astype(jnp.bfloat16)
+    up_all[prompt] = up_own[...]
+    up_start()
     weight_fetch.wait()
+    for offset in range(1, n):
+        latent_copy(offset).wait_send()
 
     sum_finish()
     token_sum = sum_all[0]
@@ -542,11 +592,13 @@
     down_total = down_all[0].astype(jnp.float32)
     for index in range(1, prompts):
         down_total = down_total + down_all[index].astype(jnp.float32)
-    down_sum[...] = down_total / prompts
+    key_down_grad[...] = down_total[:rank] / prompts
+    value_down_grad[...] = down_total[rank:] / prompts
 
     lax.fori_loop(slices // 2, slices + lag, hidden_step, 0)
     rows_finish()
-    up_sum[...] = rows_all[...].astype(jnp.float32)
+    key_up_grad[...] = rows_all[: n // 2].astype(jnp.float32).reshape(key_up_grad.shape)
+    value_up_grad[...] = rows_all[n // 2 :].astype(jnp.float32).reshape(value_up_grad.shape)
 
 
 def tail(
@@ -555,8 +607,8 @@
     normed,
     scale,
     gain,
-    down,
-    latent,
+    key_down,
+    value_down,
     key_grad,
     value_grad,
     out_weight,
@@ -580,11 +632,13 @@
         out_shape=(
             jax.ShapeDtypeStruct((length, features), low),
             jax.ShapeDtypeStruct((block, hidden), low),
-            jax.ShapeDtypeStruct((pair, features), jnp.float32),
-            jax.ShapeDtypeStruct((n, share, columns), jnp.float32),
+            jax.ShapeDtypeStruct((pair // 2, features), jnp.float32),
+            jax.ShapeDtypeStruct((pair // 2, features), jnp.float32),
+            jax.ShapeDtypeStruct((pair // 2, columns), jnp.float32),
+            jax.ShapeDtypeStruct((pair // 2, columns), jnp.float32),
         ),
         in_specs=[vmem] * 7 + [hbm] * 3,
-        out_specs=(vmem,) * 4,
+        out_specs=(vmem,) * 6,
         scratch_shapes=[
             pltpu.VMEM(out_weight.shape, low),
             pltpu.VMEM(key_grad.shape, low),
@@ -599,13 +653,15 @@
             pltpu.VMEM((prompts, pair, features), low),
             pltpu.VMEM((share, columns), low),
             pltpu.VMEM((n, share, columns), low),
+            pltpu.VMEM((n, share, length), low),
+            pltpu.VMEM((n, share, length), low),
         ]
         + [buffer] * 5
         + [dma, dma]
         + [dma((splits,))] * 4
         + [dma((n,))] * 2
         + [dma((prompts,))] * 4
-        + [dma((n,))] * 2
+        + [dma((n,))] * 4
         + [dma((slices, n))] * 4,
         compiler_params=pltpu.CompilerParams(
             collective_id=1, has_side_effects=True, vmem_limit_bytes=60 * 1024 * 1024
@@ -617,8 +673,8 @@
         normed,
         scale,
         gain,
-        down,
-        latent,
+        key_down,
+        value_down,
         key_grad,
         value_grad,
         out_weight,
@@ -641,18 +697,6 @@
     value_up,
     out_weight,
 ):
-    context = (normed[0].astype(jnp.float32) * norm_gain).astype(jnp.bfloat16)
-    latent_part = jnp.concatenate(
-        [
-            jnp.dot(context, key_down, preferred_element_type=jnp.float32),
-            jnp.dot(context, value_down, preferred_element_type=jnp.float32),
-        ],
-        axis=1,
-    )
-    latent = lax.psum(latent_part.astype(jnp.bfloat16), "seq")
-    n = lax.axis_size("seq")
-    rank = key_down.shape[1]
-    share = 2 * rank // n
     grad_query, key_grad, value_grad, context_part, project_part = attention_grads(
         queries[0],
         keys[0],
@@ -663,28 +707,26 @@
         key_up,
         value_up,
     )
-    latent_rows = lax.dynamic_slice_in_dim(latent.T, lax.axis_index("seq") * share, share, 0)
-    grad_text, grad_hidden, down_sum, up_sum = tail(
+    grad_text, grad_hidden, down_key, down_value, up_key, up_value = tail(
         context_part,
         project_part,
         normed[0],
         norm_scale[0][:, None],
         norm_gain[None, :],
-        jnp.concatenate([key_down, value_down], axis=1),
-        latent_rows,
+        key_down,
+        value_down,
         key_grad,
         value_grad,
         out_weight,
     )
-    up_rows = up_sum.reshape(2 * rank, up_sum.shape[2])
     return (
         grad_query[None],
         grad_text[None],
         grad_hidden[None],
-        down_sum[:rank].T,
-        up_rows[:rank],
-        down_sum[rank:].T,
-        up_rows[rank:],
+        down_key.T,
+        up_key,
+        down_value.T,
+        up_value,
     )
 
 

time: 294 us -> 264 us (0.90)
  Pallas kernels: 263 us -> 248 us
  between operations: 14.1 us -> 0.69 us
  matrix products: 3.42 us -> 0 us
  local copies, waits for them, and re-layouts: 11.8 us -> 15 us
    pallas_call x1, Pallas kernels: 150 us -> 135 us  [attention_grads(): pl.pallas_call(functools.partial(attention_kernel, n, heads, lag), grid=(...]
    unnamed x23 -> x29, local copies, waits for them, and re-layouts: 5.96 us -> 13.5 us
    dot_general x2 -> x0, matrix products: 3.42 us -> none  [the longest x1 1.77 us: shards(): jnp.dot(context, key_down, preferred_element_type=jnp.float32)]
  transfers between devices with their start and end apart: 1 -> 0, of which waited for: 0 -> 0; matrix products, arithmetic and copies ran while one was open for 1% -> 0% of each run, Pallas kernels for 51% -> 0%
where the time goes in v3:
time: 264 us; the launch traced here: 263 us
  Pallas kernels  248 us (94%)
  local copies, waits for them, and re-layouts  15 us (6%)
    pallas_call x1, Pallas kernels, attention_grads(): pl.pallas_call(functools.partial(attention_kernel, n, heads, lag), grid=(...  135 us
    pallas_call x1, Pallas kernels, tail(): pl.pallas_call(functools.partial(tail_kernel, n, splits, prompts, slices,...  113 us
    unnamed x29, local copies, waits for them, and re-layouts  13.5 us

profile of v3, /device:TPU:0, one launch (start us, length us, event | category | flops | bytes accessed | tf_op | source)
XLA Modules:
  0.0 263.5 jit_solution(10407240124288300925)
XLA Ops:
  0.6 1.5 copy.23.scale
  2.2 1.7 copy.24.key_down
  3.8 1.7 copy.25.value_down
  5.5 0.0 copy-start.2
  5.5 0.9 copy-done.2
  6.4 0.0 copy-start.3
  6.4 0.9 copy-done.3
  7.4 134.8 %attention.1 = (bf16[512,2560]{1,0:T(8,128)(2,1)S(1)}, bf16[512,2560]{1,0:T(8,128)(2,1)}, bf16[512,2560]{1,0:T(8,128)(2,1)}, bf16[512,1024]{1,0:T(8,128)(2,1)S(1)}, bf16[512,64]{1,0:T(8,128)(2,1)S(1)}) custom-call(bf16[512,2560]{1,0:T(8,128)(2,1)} %bitcast.20, bf16[512,2560]{1,0:T(8,128)(2,1)} %bitcast.21, bf16[512,2560]{1,0:T(8,128)(2,1)} %bitcast.22, ...), custom_call_target="tpu_custom_call" | custom-call | flops 9395240960 | bytes 15728640 | tf_op jit(solution)/shard_map/attention/pallas_call | solution.py:212
  142.2 0.0 copy-start
  142.2 1.0 copy-done
  143.1 0.0 copy-start.1
  143.1 0.7 copy-done.1
  143.8 113.0 %tail.1 = (bf16[512,1024]{1,0:T(8,128)(2,1)}, bf16[128,5120]{1,0:T(8,128)(2,1)}, f32[32,1024]{1,0:T(8,128)}, f32[32,1024]{1,0:T(8,128)}, f32[32,2560]{1,0:T(8,128)}, /*index=5*/f32[32,2560]{1,0:T(8,128)}) custom-call(bf16[512,1024]{1,0:T(8,128)(2,1)} %copy-done, bf16[512,64]{1,0:T(8,128)(2,1)} %copy-done.1, bf16[512,1024]{1,0:T(8,128)(2,1)} %bitcast.14, ...), custom_call_target="tpu_custom_call" | custom-call | tf_op jit(solution)/shard_map/tail/pallas_call | solution.py:630
  256.8 0.0 copy-start.5
  256.8 0.0 copy-start.4
  256.8 1.5 copy.33
  258.3 0.4 copy-done.5
  258.7 0.0 copy-start.9
  258.7 0.0 copy-start.7
  258.7 0.0 copy-start.8
  258.7 0.0 copy-start.6
  258.7 1.0 copy.34
  259.7 0.0 copy-done.4
  259.7 1.1 copy.35
  260.7 0.0 copy-done.9
  260.7 0.7 copy.36
  261.4 0.0 copy-done.7
  261.4 0.7 copy.37
  262.1 0.0 copy-done.8
  262.1 0.7 copy.38
  262.8 0.0 copy-done.6
  262.8 0.7 copy.39
Async XLA Ops:
  5.5 0.9 copy-start.2
  6.4 0.9 copy-start.3
  142.2 1.0 copy-start
  143.1 0.7 copy-start.1
  256.8 1.9 copy-start.5
  256.8 2.9 %copy-start.4 = (bf16[128,5120]{1,0:T(8,128)(2,1)S(1)}, bf16[128,5120]{1,0:T(8,128)(2,1)}, u32[]{:S(2)}) copy-start(bf16[128,5120]{1,0:T(8,128)(2,1)} %get-tuple-element.24) | copy-start | bytes 3932164
  258.7 2.0 copy-start.9
  258.7 2.7 %copy-start.7 = (f32[32,2560]{1,0:T(8,128)S(1)}, f32[32,2560]{1,0:T(8,128)}, u32[]{:S(2)}) copy-start(f32[32,2560]{1,0:T(8,128)} %get-tuple-element.40) | copy-start | bytes 983044
  258.7 3.4 %copy-start.8 = (f32[32,1024]{1,0:T(8,128)S(1)}, f32[32,1024]{1,0:T(8,128)}, u32[]{:S(2)}) copy-start(f32[32,1024]{1,0:T(8,128)} %get-tuple-element.27) | copy-start | bytes 393220
  258.7 4.1 %copy-start.6 = (f32[32,2560]{1,0:T(8,128)S(1)}, f32[32,2560]{1,0:T(8,128)}, u32[]{:S(2)}) copy-start(f32[32,2560]{1,0:T(8,128)} %get-tuple-element.42) | copy-start | bytes 983044
